TPU v7x, 32 devices: a whole 2x2x4 slice. The times are simulated.
32 devices in a mesh: groups: 2 (over y), seg: 4 (over z), ch: 2 (over x), sub: 2 (over core).
Axes of the slice: x: 2, y: 2, z: 4, core: 2. Of those that a mesh axis runs over, the one named last changes fastest.
Arguments:
- rank_series: bfloat16 [2048, 16384], P(('groups', 'ch', 'sub'), 'seg'), parts along dimension 0, may hold values from -6 to 6
- power_series: bfloat16 [2048, 16384], P(('groups', 'ch', 'sub'), 'seg'), parts along dimension 0, may hold values from -6 to 6
- seg_offsets: int32 [32], P(('groups', 'seg')), parts along dimension 0, may hold values from 2048 to 4095, as said below
- bin_index: int32 [128], replicated, may hold values from 0 to 511, as said below
Outputs:
- cross_spectra: bfloat16 [2, 256, 1024, 1024], P(None, ('groups', 'seg'), ('ch', 'sub')), parts along dimension 1
There are 2 independent parts, one for each index of `groups`. A program takes and returns all parts, laid end to end along the dimension named above; an argument that names none is the same for every part. Nothing has to cross between parts.
Inputs may be any that keep to these rules, and one draw needn't show every extreme that they name: `seg_offsets`: every segment reads at least half of its samples past its own 4096 samples, in the following ones. `bin_index`: the bins are distinct.
All inputs are finite; a program needn't handle non-finite values.
Results may differ from a plain program's by a relative error of at most 0.0055.
Values may be sent and summed in bfloat16 or wider, within the bound.
A program may use at most 192 MiB of HBM per device.

v0:
```python
import math

import jax
import jax.numpy as jnp
from jax import lax
from jax.sharding import PartitionSpec as P


def shifted(array, axis, by):
    peers = lax.axis_size(axis)
    pairs = [(i, i + by) for i in range(peers) if 0 <= i + by < peers]
    return lax.ppermute(array, axis, pairs)


def make_kernel(bin_index, length):
    sample_ids = jnp.arange(length, dtype=jnp.int32)
    window = 0.5 - 0.5 * jnp.cos(2.0 * math.pi / length * sample_ids.astype(jnp.float32))
    phase = bin_index[:, None] * sample_ids[None, :] % length
    angle = 2.0 * math.pi / length * phase.astype(jnp.float32)
    factor = (3.0 * length / 8.0) ** (-0.5)
    waves = jnp.stack([jnp.cos(angle), -jnp.sin(angle)]) * factor
    return (waves * window).astype(jnp.bfloat16)


def cut_segments(extended, offsets, length):

    def one_segment(offset):
        return lax.dynamic_slice_in_dim(extended, offset, length, 1)

    return jax.vmap(one_segment)(offsets)


def transform(segments, kernel):
    return jnp.einsum("tkn,scn->stkc", kernel, segments, preferred_element_type=jnp.float32)


def body(rank_series, power_series, seg_offsets, bin_index):
    length = rank_series.shape[1]
    rank_width = rank_series.shape[0]
    series_all = jnp.concatenate([rank_series, power_series], axis=0)
    kernel = make_kernel(bin_index, length)
    next_rim = shifted(series_all, "seg", -1)
    extended = jnp.concatenate([series_all, next_rim], axis=1)
    spectra = transform(cut_segments(extended, seg_offsets, length), kernel)
    spectra = spectra.astype(jnp.bfloat16)
    owned = lax.all_to_all(spectra, "seg", split_axis=2, concat_axis=0, tiled=True)
    rank_owned = owned[..., :rank_width]
    power_owned = owned[..., rank_width:]
    power_piece = lax.all_gather(power_owned, ("ch", "sub"), axis=3, tiled=True)
    swapped = jnp.concatenate([power_piece[:, 1:2], -power_piece[:, 0:1]], axis=1)
    real_part = jnp.einsum(
        "gtkr,gtkp->krp", rank_owned, power_piece, preferred_element_type=jnp.float32
    )
    imag_part = jnp.einsum(
        "gtkr,gtkp->krp", rank_owned, swapped, preferred_element_type=jnp.float32
    )
    return jnp.stack([real_part, imag_part]).astype(jnp.bfloat16)


def solution(mesh):
    return jax.shard_map(
        body,
        mesh=mesh,
        in_specs=(
            P(("groups", "ch", "sub"), "seg"),
            P(("groups", "ch", "sub"), "seg"),
            P(("groups", "seg")),
            P(),
        ),
        out_specs=P(None, ("groups", "seg"), ("ch", "sub"), None),
        check_vma=False,
    )
```

profile of v0, /device:TPU:0, one launch (start us, length us, event | category | flops | bytes accessed | tf_op | source)
XLA Modules:
  0.0 261.1 jit_solution(1151138796967690156)
XLA Ops:
  6.5 3.3 %constant_dynamic-update-slice_fusion.1 = bf16[512,4096]{1,0:T(8,128)(2,1)} fusion(bf16[256,4096]{1,0:T(8,128)(2,1)} %param.4), kind=kLoop, calls=%fused_computation.35 | loop fusion | bytes 4194304
  9.8 1.4 constant_dynamic-update-slice_fusion
  11.3 1.3 collective-permute-start
  12.6 0.1 subtract_multiply_fusion
  12.7 9.7 %fusion.27 = (f32[1,128,4096]{2,1,0:T(8,128)S(1)}, f32[1,128,4096]{2,1,0:T(8,128)}) fusion(s32[128]{0:T(128)S(1)} %copy-done.2), kind=kLoop, calls=%fused_computation.30 | loop fusion | flops 7864320 | bytes 4194816 | tf_op jit(solution)/shard_map/cos | solution.py:21
  22.4 84.7 %collective-permute-done = bf16[512,4096]{1,0:T(8,128)(2,1)} collective-permute-done((bf16[512,4096]{1,0:T(8,128)(2,1)}, bf16[512,4096]{1,0:T(8,128)(2,1)}, u32[]{:S(2)}, u32[]{:S(2)}) %collective-permute-start) | collective-permute-done | bytes 4194336 | tf_op jit(solution)/shard_map/ppermute | solution.py:12
  107.1 7.7 %pad_maximum_fusion.1 = bf16[512,8192]{1,0:T(8,128)(2,1)} fusion(bf16[512,4096]{1,0:T(8,128)(2,1)} %collective-permute-done, bf16[512,4096]{1,0:T(8,128)(2,1)} %constant_dynamic-update-slice_fusion), kind=kLoop, calls=%fused_computation.9 | loop fusion | flops 16777216 | bytes 16777216 | tf_op jit(solution)/shard_map/concatenate | solution.py:43
  114.8 32.7 %while.1 = (s32[]{:T(128)}, bf16[512,8192]{1,0:T(8,128)(2,1)}, s32[4,2]{0,1:T(2,128)S(1)}, bf16[4,512,4096]{2,1,0:T(8,128)(2,1)}, s32[]{:T(128)}) while((s32[]{:T(128)}, bf16[512,8192]{1,0:T(8,128)(2,1)}, s32[4,2]{0,1:T(2,128)S(1)}, bf16[4,512,4096]{2,1,0:T(8,128)(2,1)}, s32[]{:T(128)}) %tuple.18), condition=%wide.while_cond, body=%wide.while_body.sunk | while | flops 2 | bytes 8389221 | solution.py:28
  114.8 0.1 constant_dynamic-slice_fusion.2
  114.8 0.6 slice.38
  115.4 7.5 %bitcast_dynamic-update-slice_fusion.2 = bf16[4,512,4096]{2,1,0:T(8,128)(2,1)} fusion(bf16[4,512,4096]{2,1,0:T(8,128)(2,1)} %get-tuple-element.58, s32[]{:T(128)S(6)} %copy.18, bf16[512,8192]{1,0:T(8,128)(2,1)} %get-tuple-element.61, s32[]{:T(128)} %bitcast.46), kind=kLoop, calls=%fused_computation.clone.1 | loop fusion | bytes 8389124 | tf_op jit(solution)/shard_map/vmap()/gather
  122.9 0.1 constant_dynamic-slice_fusion.2
  123.0 0.6 slice.38
  123.6 7.5 %bitcast_dynamic-update-slice_fusion.2 = bf16[4,512,4096]{2,1,0:T(8,128)(2,1)} fusion(bf16[4,512,4096]{2,1,0:T(8,128)(2,1)} %get-tuple-element.58, s32[]{:T(128)S(6)} %copy.18, bf16[512,8192]{1,0:T(8,128)(2,1)} %get-tuple-element.61, s32[]{:T(128)} %bitcast.46), kind=kLoop, calls=%fused_computation.clone.1 | loop fusion | bytes 8389124 | tf_op jit(solution)/shard_map/vmap()/gather
  131.1 0.1 constant_dynamic-slice_fusion.2
  131.2 0.6 slice.38
  131.8 7.5 %bitcast_dynamic-update-slice_fusion.2 = bf16[4,512,4096]{2,1,0:T(8,128)(2,1)} fusion(bf16[4,512,4096]{2,1,0:T(8,128)(2,1)} %get-tuple-element.58, s32[]{:T(128)S(6)} %copy.18, bf16[512,8192]{1,0:T(8,128)(2,1)} %get-tuple-element.61, s32[]{:T(128)} %bitcast.46), kind=kLoop, calls=%fused_computation.clone.1 | loop fusion | bytes 8389124 | tf_op jit(solution)/shard_map/vmap()/gather
  139.3 0.1 constant_dynamic-slice_fusion.2
  139.4 0.6 slice.38
  139.9 7.5 %bitcast_dynamic-update-slice_fusion.2 = bf16[4,512,4096]{2,1,0:T(8,128)(2,1)} fusion(bf16[4,512,4096]{2,1,0:T(8,128)(2,1)} %get-tuple-element.58, s32[]{:T(128)S(6)} %copy.18, bf16[512,8192]{1,0:T(8,128)(2,1)} %get-tuple-element.61, s32[]{:T(128)} %bitcast.46), kind=kLoop, calls=%fused_computation.clone.1 | loop fusion | bytes 8389124 | tf_op jit(solution)/shard_map/vmap()/gather
  147.5 8.8 %fusion.22 = bf16[4,2,128,512]{2,3,1,0:T(8,128)(2,1)S(1)} fusion(f32[1,128,4096]{2,1,0:T(8,128)} %get-tuple-element.24, f32[1,128,4096]{2,1,0:T(8,128)S(1)} %get-tuple-element.23, f32[4096]{0:T(1024)S(1)} %subtract_multiply_fusion, bf16[4,512,4096]{2,1,0:T(8,128)(2,1)} %get-tuple-element.12), kind=kOutput, calls=%fused_computation.28 | convolution fusion | flops 4298637312 | bytes 22036480 | tf_op jit(solution)/shard_map/tkn,scn->stkc/dot_general | solution.py:34
  156.3 1.0 copy.8
  157.2 28.7 %all_to_all.18 = bf16[4,2,128,512]{3,1,0,2:T(2,128)(2,1)S(1)} all-to-all(bf16[4,2,128,512]{3,1,0,2:T(2,128)(2,1)S(1)} %copy.8), channel_id=1, replica_groups=mesh['groups'=2,'seg'=4,'ch'=2,'sub'=2] {'seg'}, dimensions={2} | all-to-all | bytes 2097152 | tf_op jit(solution)/shard_map/all_to_all | solution.py:46
  185.9 0.3 copy.9
  186.2 0.8 copy.10
  187.1 0.3 all_to_all.16
  187.3 0.8 slice.28
  188.2 22.1 %all-gather.2.cloned.1.call-done = bf16[16,2,32,1024]{3,0,1,2:T(8,128)(2,1)} async-done(((bf16[16,2,32,256]{3,0,1,2:T(8,128)(2,1)}), bf16[16,2,32,1024]{3,0,1,2:T(8,128)(2,1)}) %all-gather.2.cloned.1.call-update) | async-done | bytes 2097168 | tf_op jit(solution)/shard_map/all_gather | solution.py:49
  210.3 3.0 %fusion.33 = (bf16[16,1,32,1024]{3,0,1,2:T(8,128)(2,1)}, bf16[16,1,32,1024]{3,0,1,2:T(8,128)(2,1)}) fusion(bf16[16,2,32,1024]{3,0,1,2:T(8,128)(2,1)} %all-gather.2.cloned.1.call-done), kind=kLoop, calls=%fused_computation.40 | loop fusion | flops 524288 | bytes 4194304 | tf_op jit(solution)/shard_map/slice | solution.py:50
  213.3 9.8 %fusion.1 = bf16[1,32,256,1024]{3,2,1,0:T(8,128)(2,1)} fusion(bf16[16,1,32,1024]{3,0,1,2:T(8,128)(2,1)} %get-tuple-element.22, bf16[16,1,32,1024]{3,0,1,2:T(8,128)(2,1)} %get-tuple-element.21, bf16[16,2,32,512]{3,0,1,2:T(8,128)(2,1)S(1)} %all_to_all.16), kind=kOutput, calls=%fused_computation.6 | convolution fusion | flops 546308096 | bytes 19398656 | tf_op jit(solution)/shard_map/gtkr,gtkp->krp/dot_general | solution.py:54
  223.1 8.1 %fusion = bf16[1,32,256,1024]{3,2,1,0:T(8,128)(2,1)} fusion(bf16[16,2,32,1024]{3,0,1,2:T(8,128)(2,1)S(1)} %copy-done, bf16[16,2,32,512]{3,0,1,2:T(8,128)(2,1)S(1)} %all_to_all.16), kind=kOutput, calls=%fused_computation.5 | convolution fusion | flops 545259520 | bytes 19398656 | tf_op jit(solution)/shard_map/gtkr,gtkp->krp/dot_general | solution.py:51
  231.2 23.0 %pad_maximum_fusion = bf16[2,32,256,1024]{3,2,1,0:T(8,128)(2,1)} fusion(bf16[1,32,256,1024]{3,2,1,0:T(8,128)(2,1)} %fusion.1, bf16[1,32,256,1024]{3,2,1,0:T(8,128)(2,1)} %fusion), kind=kLoop, calls=%fused_computation.2 | loop fusion | flops 16777216 | bytes 67108864 | tf_op jit(solution)/shard_map/stack | solution.py:57
  (13 shorter events, 0.0 us)
Async XLA Ops:
  6.5 3.3 %copy-start.1 = (bf16[256,4096]{1,0:T(8,128)(2,1)S(1)}, bf16[256,4096]{1,0:T(8,128)(2,1)}, u32[]{:S(2)}) copy-start(bf16[256,4096]{1,0:T(8,128)(2,1)} %param.5) | copy-start | bytes 6291460
  6.5 6.0 %copy-start.3 = (s32[4]{0:T(128)S(1)}, s32[4]{0:T(128)}, u32[]{:S(2)}) copy-start(s32[4]{0:T(128)} %param.6) | copy-start | bytes 52
  6.5 6.1 %copy-start.2 = (s32[128]{0:T(128)S(1)}, s32[128]{0:T(128)}, u32[]{:S(2)}) copy-start(s32[128]{0:T(128)} %param.7) | copy-start | bytes 1540
  6.5 203.8 %all-gather.2.cloned.1.call-start = ((), (), s32[]{:S(2)}) async-start(), calls=%async_computation.1 | async-start | bytes 2621440 | tf_op jit(solution)/shard_map/all_gather | solution.py:49
  11.3 95.8 %collective-permute-start = (bf16[512,4096]{1,0:T(8,128)(2,1)}, bf16[512,4096]{1,0:T(8,128)(2,1)}, u32[]{:S(2)}, u32[]{:S(2)}) collective-permute-start(bf16[512,4096]{1,0:T(8,128)(2,1)} %constant_dynamic-update-slice_fusion), channel_id=1, source_target_pairs={{4,0},{8,4},{12,8},{5,1},{9,5},{13,9},{6,2},{10,6},{14,10},{7,3},{... | collective-permute-start | bytes 12582920 | tf_op jit(solution)/shard_map/ppermute | solution.py:12
  213.3 9.8 %copy-start = (bf16[16,2,32,1024]{3,0,1,2:T(8,128)(2,1)S(1)}, bf16[16,2,32,1024]{3,0,1,2:T(8,128)(2,1)}, u32[]{:S(2)}) copy-start(bf16[16,2,32,1024]{3,0,1,2:T(8,128)(2,1)} %all-gather.2.cloned.1.call-done) | copy-start | bytes 6291460
Sparse Core Ops, SparseCore 0:
  188.3 21.9 all-gather.1
where the time goes:
time: 261 us
  waiting for transfers between devices  107 us (41%)
  other arithmetic  43.4 us (17%)
  local copies, waits for them, and re-layouts  40.7 us (16%)
  blocking collectives  28.7 us (11%)
  matrix products  26.7 us (10%)
  between operations  13.5 us (5%)
    ppermute x1, waiting for transfers between devices, shifted(): return lax.ppermute(array, axis, pairs)  84.7 us
    gather x12, local copies, waits for them, and re-layouts  32.7 us
    all_to_all x1, blocking collectives, body(): lax.all_to_all(spectra, 'seg', split_axis=2, concat_axis=0, tiled=True)  28.7 us
    another operation x1, other arithmetic, body(): return jnp.stack([real_part, imag_part]).astype(jnp.bfloat16)  23 us
    all_gather x1, waiting for transfers between devices, body(): power_piece = lax.all_gather(power_owned, ('ch', 'sub'), axis=3, tiled=True)  22.1 us
    dot_general x1, matrix products, body(): jnp.einsum('gtkr,gtkp->krp', rank_owned, swapped, preferred_element_type=...  9.81 us
    cos x1, other arithmetic, make_kernel(): waves = jnp.stack([jnp.cos(angle), -jnp.sin(angle)]) * factor  9.69 us
    dot_general x1, matrix products, transform(): jnp.einsum('tkn,scn->stkc', kernel, segments, preferred_element_type=jnp....  8.77 us
  transfers between devices with their start and end apart: 2, of which 2 were waited for; matrix products, arithmetic and copies ran while one was open for 4% of the time, Pallas kernels for 0%

commit v1 on v0

v1 whole, which is shorter than its diff:
```python
import functools
import math

import jax
import jax.numpy as jnp
from jax import lax
from jax.experimental import pallas as pl
from jax.experimental.pallas import tpu as pltpu
from jax.sharding import PartitionSpec as P

LANES = 128
FINE = 64


def shifted(array, axis, by):
    peers = lax.axis_size(axis)
    pairs = [(i, i + by) for i in range(peers) if 0 <= i + by < peers]
    return lax.ppermute(array, axis, pairs)


def waves_of(bin_index, samples, length):
    freqs = jnp.stack([bin_index, jnp.ones_like(bin_index)])
    phase = freqs[:, None, :] * samples[None, :, None] % length
    angle = 2.0 * math.pi / length * phase.astype(jnp.float32)
    return jnp.stack([jnp.cos(angle), jnp.sin(angle)])


def spectra_kernel(
    length, head, chunk, off_ref, grid_ref, back_ref, rank_ref, power_ref, rank_out, power_out, acc, stage
):
    bins = grid_ref.shape[-1]
    width = rank_ref.shape[0]
    segs = off_ref.shape[0]
    first = 0 if head else length // 2
    coarse = length // FINE
    factor = (3.0 * length / 8.0) ** (-0.5)

    for g in range(segs):
        offset = off_ref[g]
        acc[...] = jnp.zeros_like(acc)
        moved = []
        for kind in range(2):
            cb = grid_ref[0, kind, coarse : coarse + FINE, :]
            sb = grid_ref[1, kind, coarse : coarse + FINE, :]
            co = back_ref[0, kind, g : g + 1, :]
            so = back_ref[1, kind, g : g + 1, :]
            moved.append((cb * co - sb * so, sb * co + cb * so))

        @pl.loop(0, (length - first) // chunk)
        def _(c):
            rows = []
            for piece in range(chunk // FINE):
                a = first // FINE + c * (chunk // FINE) + piece
                ca = grid_ref[0, 0, pl.ds(a, 1), :]
                sa = grid_ref[1, 0, pl.ds(a, 1), :]
                cw = grid_ref[0, 1, pl.ds(a, 1), :]
                sw = grid_ref[1, 1, pl.ds(a, 1), :]
                (cb, sb), (cv, sv) = moved
                window = (0.5 - 0.5 * (cw * cv - sw * sv)) * factor
                sample = lax.broadcasted_iota(jnp.int32, (FINE, bins), 0) + a * FINE
                inside = sample < offset if head else sample >= offset
                window = jnp.where(inside, window, 0.0)
                cosine = (ca * cb - sa * sb) * window
                sine = (sa * cb + ca * sb) * -window
                rows.append(jnp.concatenate([cosine, sine], axis=1).astype(jnp.bfloat16))
            col = pl.multiple_of(first + c * chunk, chunk)
            series = jnp.concatenate(
                [rank_ref[:, pl.ds(col, chunk)], power_ref[:, pl.ds(col, chunk)]], axis=0
            )
            acc[...] += jnp.dot(
                series, jnp.concatenate(rows, axis=0), preferred_element_type=jnp.float32
            )

        for t in range(2):
            for l in range(2 * width // LANES):
                part = acc[l * LANES : (l + 1) * LANES, t * bins : (t + 1) * bins]
                stage[l, pl.ds(t * segs + g, bins, stride=2 * segs), :] = part.T

    per = width // LANES
    for l in range(2 * per):
        out = rank_out if l < per else power_out
        lane = (l % per) * LANES
        out[:, :, lane : lane + LANES] = (
            stage[l].reshape(bins, 2 * segs, LANES).astype(out.dtype)
        )


def spectra(offsets, grid, bin_index, rank_series, power_series, head):
    width, length = rank_series.shape
    bins = grid.shape[-1]
    segs = offsets.shape[0]
    back = waves_of(bin_index, -offsets, length)
    dtype = jnp.bfloat16 if head else jnp.float32
    out = jax.ShapeDtypeStruct((bins, 2 * segs, width), dtype)
    rows = length if head else length // 2
    vmem = pl.BlockSpec(memory_space=pltpu.VMEM)
    return pl.pallas_call(
        functools.partial(spectra_kernel, length, head, 1024),
        out_shape=(out, out),
        in_specs=[pl.BlockSpec(memory_space=pltpu.SMEM), vmem, vmem, vmem, vmem],
        out_specs=(vmem, vmem),
        scratch_shapes=[
            pltpu.VMEM((2 * width, 2 * bins), jnp.float32),
            pltpu.VMEM((2 * width // LANES, bins * 2 * segs, LANES), jnp.float32),
        ],
        compiler_params=pltpu.CompilerParams(vmem_limit_bytes=40 << 20),
        cost_estimate=pl.CostEstimate(
            flops=2 * segs * rows * 2 * bins * 2 * width,
            bytes_accessed=2 * width * length * 2,
            transcendentals=0,
        ),
        name="head_spectra" if head else "own_spectra",
    )(offsets, grid, back, rank_series, power_series)


def cross_kernel(rank_ref, power_ref, out_ref):
    peers, block, rows, width = rank_ref.shape
    gathered = power_ref.shape[0]
    half = rows // 2
    depth = peers * rows
    for i in range(block):
        rank = rank_ref[:, i].astype(jnp.float32)
        turned = jnp.concatenate([-rank[:, half:], rank[:, :half]], axis=1)
        both = jnp.concatenate([rank.reshape(depth, width), turned.reshape(depth, width)], axis=1)
        both = both.astype(jnp.bfloat16)
        for d in range(gathered):
            power = power_ref[d, :, i].astype(jnp.float32).reshape(depth, width)
            sums = lax.dot_general(
                both,
                power.astype(jnp.bfloat16),
                (((0,), (0,)), ((), ())),
                preferred_element_type=jnp.float32,
            ).astype(out_ref.dtype)
            out_ref[0, i, :, d * width : (d + 1) * width] = sums[:width]
            out_ref[1, i, :, d * width : (d + 1) * width] = sums[width:]


def cross(rank_owned, power_all):
    peers, bins, rows, width = rank_owned.shape
    gathered = power_all.shape[0]
    block = 2
    return pl.pallas_call(
        cross_kernel,
        out_shape=jax.ShapeDtypeStruct((2, bins, width, gathered * width), jnp.bfloat16),
        grid=(bins // block,),
        in_specs=[
            pl.BlockSpec((peers, block, rows, width), lambda k: (0, k, 0, 0)),
            pl.BlockSpec((gathered, peers, block, rows, width), lambda k: (0, 0, k, 0, 0)),
        ],
        out_specs=pl.BlockSpec((2, block, width, gathered * width), lambda k: (0, k, 0, 0)),
        compiler_params=pltpu.CompilerParams(vmem_limit_bytes=48 << 20),
        name="cross_spectra",
    )(rank_owned, power_all)


def to_owners(array):
    peers = lax.axis_size("seg")
    split = array.reshape((peers, array.shape[0] // peers) + array.shape[1:])
    return lax.all_to_all(split, "seg", split_axis=0, concat_axis=0)


def body(rank_series, power_series, seg_offsets, bin_index):
    length = rank_series.shape[1]
    coarse = jnp.arange(0, length, FINE, dtype=jnp.int32)
    samples = jnp.concatenate([coarse, jnp.arange(FINE, dtype=jnp.int32)])
    grid = waves_of(bin_index, samples, length)
    before = shifted(seg_offsets, "seg", 1)
    rank_head, power_head = spectra(before, grid, bin_index, rank_series, power_series, True)
    power_head = shifted(power_head, "seg", -1)
    rank_head = shifted(rank_head, "seg", -1)
    rank_own, power_own = spectra(seg_offsets, grid, bin_index, rank_series, power_series, False)
    power_spectra = (power_own + power_head.astype(jnp.float32)).astype(jnp.bfloat16)
    rank_spectra = (rank_own + rank_head.astype(jnp.float32)).astype(jnp.bfloat16)
    power_all = lax.all_gather(to_owners(power_spectra), ("ch", "sub"), axis=0)
    return cross(to_owners(rank_spectra), power_all)


def solution(mesh):
    return jax.shard_map(
        body,
        mesh=mesh,
        in_specs=(
            P(("groups", "ch", "sub"), "seg"),
            P(("groups", "ch", "sub"), "seg"),
            P(("groups", "seg")),
            P(),
        ),
        out_specs=P(None, ("groups", "seg"), ("ch", "sub"), None),
        check_vma=False,
    )
```

time: 261 us -> 116 us (0.44)
  waiting for transfers between devices: 107 us -> 20.2 us
  other arithmetic: 43.4 us -> 1.77 us
  Pallas kernels: 0 us -> 35.7 us
  local copies, waits for them, and re-layouts: 40.7 us -> 5.43 us
  matrix products: 26.7 us -> 0 us
  starting transfers between devices: 1.28 us -> 7.5 us
  blocking collectives: 28.7 us -> 32 us
    ppermute x1 -> x3, waiting for transfers between devices: 84.7 us -> 20.2 us  [shifted(): return lax.ppermute(array, axis, pairs)]
    pallas_call x0 -> x3, Pallas kernels: none -> 35.7 us  [the longest x2 18.5 us: spectra(): pl.pallas_call(functools.partial(spectra_kernel, length, head, 1024), out...]
    gather x12 -> x0, local copies, waits for them, and re-layouts: 32.7 us -> none
    dot_general x3 -> x0, matrix products: 26.7 us -> none  [the longest x1 9.81 us: body(): jnp.einsum('gtkr,gtkp->krp', rank_owned, swapped, preferred_element_type=...]
    another operation x1 -> x2, other arithmetic: 23 us -> 0.03 us  [waves_of(): return jnp.stack([jnp.cos(angle), jnp.sin(angle)])]
    all_gather x1, waiting for transfers between devices: 22.1 us -> 0.01 us  [body(): power_all = lax.all_gather(to_owners(power_spectra), ('ch', 'sub'), axis=0)]
    cos x1 -> x2, other arithmetic: 9.69 us -> 0.74 us  [waves_of(): return jnp.stack([jnp.cos(angle), jnp.sin(angle)])]
    concatenate x1, other arithmetic: 7.68 us -> 0.08 us  [body(): samples = jnp.concatenate([coarse, jnp.arange(FINE, dtype=jnp.int32)])]
  transfers between devices with their start and end apart: 2 -> 4, of which waited for: 2 -> 2; matrix products, arithmetic and copies ran while one was open for 4% -> 2% of each run, Pallas kernels for 0% -> 6%
where the time goes in v1:
time: 116 us
  Pallas kernels  35.7 us (31%)
  blocking collectives  32 us (28%)
  waiting for transfers between devices  20.2 us (17%)
  between operations  13.5 us (12%)
  starting transfers between devices  7.5 us (6%)
  local copies, waits for them, and re-layouts  5.43 us (5%)
  other arithmetic  1.77 us (2%)
    all_to_all x2, blocking collectives, to_owners(): return lax.all_to_all(split, 'seg', split_axis=0, concat_axis=0)  32 us
    ppermute x3, waiting for transfers between devices, shifted(): return lax.ppermute(array, axis, pairs)  20.2 us
    pallas_call x2, Pallas kernels, spectra(): pl.pallas_call(functools.partial(spectra_kernel, length, head, 1024), out...  18.5 us
    pallas_call x1, Pallas kernels, cross(): pl.pallas_call(cross_kernel, out_shape=jax.ShapeDtypeStruct((2, bins, wid...  17.3 us
    ppermute x3, starting transfers between devices, shifted(): return lax.ppermute(array, axis, pairs)  7.5 us
    unnamed x8, local copies, waits for them, and re-layouts  4.77 us
  transfers between devices with their start and end apart: 4, of which 2 were waited for; matrix products, arithmetic and copies ran while one was open for 2% of the time, Pallas kernels for 6%

profile of v1, /device:TPU:0, one launch (start us, length us, event | category | flops | bytes accessed | tf_op | source)
XLA Modules:
  0.0 116.1 jit_solution(8636624759336006448)
XLA Ops:
  6.5 0.0 all-gather.3.cloned.1.call-start
  6.5 4.9 %collective-permute-start = (s32[4]{0:T(128)}, s32[4]{0:T(128)S(1)}, u32[]{:S(2)}, u32[]{:S(2)}) collective-permute-start(s32[4]{0:T(128)} %off_ref.1), channel_id=1, source_target_pairs={{0,4},{4,8},{8,12},{1,5},{5,9},{9,13},{2,6},{6,10},{10,14},{3,7},{... | collective-permute-start | bytes 56 | tf_op jit(solution)/shard_map/ppermute | solution.py:18
  11.5 0.7 neg.6
  12.1 0.1 pad_add_fusion
  12.2 0.7 stack.11
  12.9 0.6 fusion.4
  13.5 0.0 collective-permute-done.off_ref
  13.5 0.2 fusion.12
  13.7 0.0 copy-start.1
  13.7 1.6 %copy-done.1 = bf16[256,4096]{1,0:T(8,128)(2,1)S(1)} copy-done((bf16[256,4096]{1,0:T(8,128)(2,1)S(1)}, bf16[256,4096]{1,0:T(8,128)(2,1)}, u32[]{:S(2)}) %copy-start.1) | copy-done | bytes 2097176
  15.3 0.0 copy-start.2
  15.3 1.6 %copy-done.2 = bf16[256,4096]{1,0:T(8,128)(2,1)S(1)} copy-done((bf16[256,4096]{1,0:T(8,128)(2,1)S(1)}, bf16[256,4096]{1,0:T(8,128)(2,1)}, u32[]{:S(2)}) %copy-start.2) | copy-done | bytes 2097176
  16.9 0.0 copy-start.3
  16.9 11.8 %head_spectra.1 = (bf16[128,8,256]{2,1,0:T(8,128)(2,1)S(1)}, bf16[128,8,256]{2,1,0:T(8,128)(2,1)S(1)}) custom-call(s32[4]{0:T(128)S(1)} %collective-permute-done.off_ref, f32[2,2,128,128]{3,2,1,0:T(8,128)S(1)} %pad_maximum_fusion.grid_ref, f32[2,2,4,128]{3,2,1,0:T(4,128)S(1)} %get-tuple-element.22.back_ref, bf16[256,4096]{1,0:T(8,128)(2,1)S(1)} %copy-done.1, ...), custom_call_target="tpu_custom_call" | custom-call | flops 4294967296 | bytes 4194304 | tf_op jit(solution)/shard_map/head_spectra/pallas_call | solution.py:97
  28.7 1.3 %collective-permute-start.2 = (bf16[128,8,256]{2,1,0:T(8,128)(2,1)S(1)}, bf16[128,8,256]{2,1,0:T(8,128)(2,1)S(1)}, u32[]{:S(2)}, u32[]{:S(2)}) collective-permute-start(bf16[128,8,256]{2,1,0:T(8,128)(2,1)S(1)} %get-tuple-element.12), channel_id=1, source_target_pairs={{4,0},{8,4},{12,8},{5,1},{9,5},{13,9},{6,2},{10,6},{14,10},{7,3},{... | collective-permute-start | bytes 1572872 | tf_op jit(solution)/shard_map/ppermute | solution.py:18
  30.0 0.0 copy-done.3
  30.0 6.7 %own_spectra.1 = (f32[128,8,256]{2,1,0:T(8,128)S(1)}, f32[128,8,256]{2,1,0:T(8,128)S(1)}) custom-call(s32[4]{0:T(128)S(1)} %copy-done.3, f32[2,2,128,128]{3,2,1,0:T(8,128)S(1)} %pad_maximum_fusion.grid_ref, f32[2,2,4,128]{3,2,1,0:T(4,128)S(1)} %get-tuple-element.21.back_ref, bf16[256,4096]{1,0:T(8,128)(2,1)S(1)} %copy-done.1, bf16[256,4096]{1,0:T(8,128)(2,1)S(1)} %copy-done.2), custom_call_target="tpu_custom_call" | custom-call | flops 2147483648 | bytes 4194304 | tf_op jit(solution)/shard_map/own_spectra/pallas_call | solution.py:97
  36.7 7.3 %collective-permute-done.2 = bf16[128,8,256]{2,1,0:T(8,128)(2,1)S(1)} collective-permute-done((bf16[128,8,256]{2,1,0:T(8,128)(2,1)S(1)}, bf16[128,8,256]{2,1,0:T(8,128)(2,1)S(1)}, u32[]{:S(2)}, u32[]{:S(2)}) %collective-permute-start.2) | collective-permute-done | bytes 524320 | tf_op jit(solution)/shard_map/ppermute | solution.py:18
  43.9 0.1 add_convert_fusion
  44.1 17.0 %all_to_all.10 = bf16[4,32,8,256]{3,2,1,0:T(8,128)(2,1)} all-to-all(bf16[4,32,8,256]{3,2,1,0:T(8,128)(2,1)S(1)} %bitcast.5), channel_id=1, replica_groups=mesh['groups'=2,'seg'=4,'ch'=2,'sub'=2] {'seg'}, dimensions={0} | all-to-all | bytes 1048576 | tf_op jit(solution)/shard_map/all_to_all | solution.py:159
  61.1 0.0 all-gather.3.cloned.1.call-update
  61.1 1.3 %collective-permute-start.1 = (bf16[128,8,256]{2,1,0:T(8,128)(2,1)S(1)}, bf16[128,8,256]{2,1,0:T(8,128)(2,1)S(1)}, u32[]{:S(2)}, u32[]{:S(2)}) collective-permute-start(bf16[128,8,256]{2,1,0:T(8,128)(2,1)S(1)} %get-tuple-element.10), channel_id=1, source_target_pairs={{4,0},{8,4},{12,8},{5,1},{9,5},{13,9},{6,2},{10,6},{14,10},{7,3},{... | collective-permute-start | bytes 1572872 | tf_op jit(solution)/shard_map/ppermute | solution.py:18
  62.4 12.9 %collective-permute-done.1 = bf16[128,8,256]{2,1,0:T(8,128)(2,1)S(1)} collective-permute-done((bf16[128,8,256]{2,1,0:T(8,128)(2,1)S(1)}, bf16[128,8,256]{2,1,0:T(8,128)(2,1)S(1)}, u32[]{:S(2)}, u32[]{:S(2)}) %collective-permute-start.1) | collective-permute-done | bytes 524320 | tf_op jit(solution)/shard_map/ppermute | solution.py:18
  75.3 0.1 add_convert_fusion.1
  75.5 15.0 %all_to_all.11.rank_ref = bf16[4,32,8,256]{3,2,1,0:T(8,128)(2,1)S(1)} all-to-all(bf16[4,32,8,256]{3,2,1,0:T(8,128)(2,1)S(1)} %bitcast.6), channel_id=1, replica_groups=mesh['groups'=2,'seg'=4,'ch'=2,'sub'=2] {'seg'}, dimensions={0} | all-to-all | bytes 1048576 | tf_op jit(solution)/shard_map/all_to_all | solution.py:159
  90.4 0.0 all-gather.3.cloned.1.call-done
  90.4 0.0 copy-start
  90.4 1.6 %copy-done = bf16[16,32,8,256]{3,2,1,0:T(8,128)(2,1)S(1)} copy-done((bf16[16,32,8,256]{3,2,1,0:T(8,128)(2,1)S(1)}, bf16[16,32,8,256]{3,2,1,0:T(8,128)(2,1)}, u32[]{:S(2)}) %copy-start) | copy-done | bytes 2097176
  92.0 17.3 %cross_spectra.1 = bf16[2,32,256,1024]{3,2,1,0:T(8,128)(2,1)} custom-call(bf16[4,32,8,256]{3,2,1,0:T(8,128)(2,1)S(1)} %all_to_all.11.rank_ref, bf16[4,4,32,8,256]{4,3,2,1,0:T(8,128)(2,1)S(1)} %bitcast.4), custom_call_target="tpu_custom_call" | custom-call | tf_op jit(solution)/shard_map/cross_spectra/pallas_call | solution.py:142
  (5 shorter events, 0.0 us)
Async XLA Ops:
  6.5 83.9 %all-gather.3.cloned.1.call-start = ((), (), s32[]{:S(2)}) async-start(), calls=%async_computation.2 | async-start | bytes 2621440 | tf_op jit(solution)/shard_map/all_gather | solution.py:174
  6.5 7.0 %collective-permute-start = (s32[4]{0:T(128)}, s32[4]{0:T(128)S(1)}, u32[]{:S(2)}, u32[]{:S(2)}) collective-permute-start(s32[4]{0:T(128)} %off_ref.1), channel_id=1, source_target_pairs={{0,4},{4,8},{8,12},{1,5},{5,9},{9,13},{2,6},{6,10},{10,14},{3,7},{... | collective-permute-start | bytes 56 | tf_op jit(solution)/shard_map/ppermute | solution.py:18
  13.7 1.6 %copy-start.1 = (bf16[256,4096]{1,0:T(8,128)(2,1)S(1)}, bf16[256,4096]{1,0:T(8,128)(2,1)}, u32[]{:S(2)}) copy-start(bf16[256,4096]{1,0:T(8,128)(2,1)} %rank_ref.3) | copy-start | bytes 6291460
  15.3 1.6 %copy-start.2 = (bf16[256,4096]{1,0:T(8,128)(2,1)S(1)}, bf16[256,4096]{1,0:T(8,128)(2,1)}, u32[]{:S(2)}) copy-start(bf16[256,4096]{1,0:T(8,128)(2,1)} %power_ref.3) | copy-start | bytes 6291460
  16.9 13.1 %copy-start.3 = (s32[4]{0:T(128)S(1)}, s32[4]{0:T(128)}, u32[]{:S(2)}) copy-start(s32[4]{0:T(128)} %off_ref.1) | copy-start | bytes 52
  28.7 15.3 %collective-permute-start.2 = (bf16[128,8,256]{2,1,0:T(8,128)(2,1)S(1)}, bf16[128,8,256]{2,1,0:T(8,128)(2,1)S(1)}, u32[]{:S(2)}, u32[]{:S(2)}) collective-permute-start(bf16[128,8,256]{2,1,0:T(8,128)(2,1)S(1)} %get-tuple-element.12), channel_id=1, source_target_pairs={{4,0},{8,4},{12,8},{5,1},{9,5},{13,9},{6,2},{10,6},{14,10},{7,3},{... | collective-permute-start | bytes 1572872 | tf_op jit(solution)/shard_map/ppermute | solution.py:18
  61.1 14.2 %collective-permute-start.1 = (bf16[128,8,256]{2,1,0:T(8,128)(2,1)S(1)}, bf16[128,8,256]{2,1,0:T(8,128)(2,1)S(1)}, u32[]{:S(2)}, u32[]{:S(2)}) collective-permute-start(bf16[128,8,256]{2,1,0:T(8,128)(2,1)S(1)} %get-tuple-element.10), channel_id=1, source_target_pairs={{4,0},{8,4},{12,8},{5,1},{9,5},{13,9},{6,2},{10,6},{14,10},{7,3},{... | collective-permute-start | bytes 1572872 | tf_op jit(solution)/shard_map/ppermute | solution.py:18
  90.4 1.6 %copy-start = (bf16[16,32,8,256]{3,2,1,0:T(8,128)(2,1)S(1)}, bf16[16,32,8,256]{3,2,1,0:T(8,128)(2,1)}, u32[]{:S(2)}) copy-start(bf16[16,32,8,256]{3,2,1,0:T(8,128)(2,1)} %all-gather.3.cloned.1.call-done) | copy-start | bytes 6291460
Sparse Core Ops, SparseCore 0:
  61.3 21.6 all-gather.2

commit v2 on v1

--- a/solution.py
+++ b/solution.py
@@ -25,9 +25,7 @@
     return jnp.stack([jnp.cos(angle), jnp.sin(angle)])
 
 
-def spectra_kernel(
-    length, head, chunk, off_ref, grid_ref, back_ref, rank_ref, power_ref, rank_out, power_out, acc, stage
-):
+def transform(length, head, chunk, off_ref, grid_ref, back_ref, rank_ref, power_ref, acc, stage):
     bins = grid_ref.shape[-1]
     width = rank_ref.shape[0]
     segs = off_ref.shape[0]
@@ -76,41 +74,217 @@
                 part = acc[l * LANES : (l + 1) * LANES, t * bins : (t + 1) * bins]
                 stage[l, pl.ds(t * segs + g, bins, stride=2 * segs), :] = part.T
 
+
+def head_kernel(
+    length, chunk, off_ref, grid_ref, back_ref, rank_ref, power_ref, power_out, rank_out, acc, stage
+):
+    transform(length, True, chunk, off_ref, grid_ref, back_ref, rank_ref, power_ref, acc, stage)
+    peers, block, rows, width = rank_out.shape
     per = width // LANES
     for l in range(2 * per):
         out = rank_out if l < per else power_out
         lane = (l % per) * LANES
-        out[:, :, lane : lane + LANES] = (
-            stage[l].reshape(bins, 2 * segs, LANES).astype(out.dtype)
-        )
-
-
-def spectra(offsets, grid, bin_index, rank_series, power_series, head):
+        out[:, :, :, lane : lane + LANES] = (
+            stage[l].reshape(peers, block, rows, LANES).astype(out.dtype)
+        )
+
+
+def exchange_kernel(
+    length, chunk, peers, plane, off_ref, grid_ref, back_ref, rank_ref, power_ref, power_head, rank_head,
+    power_all, rank_owned, acc, stage, arrived, summed,
+    head_send, head_recv, own_send, own_recv, plane_send, plane_recv,
+):
+    mesh_id = pl.DeviceIdType.MESH
+    here = lax.axis_index("seg")
+    fanout = plane[0] * plane[1]
+    place = lax.axis_index("ch") * plane[1] + lax.axis_index("sub")
+    block, rows, width = summed.shape[2:]
+    per = width // LANES
+
+    def along(z):
+        return {"seg": z}
+
+    def beside(q):
+        return {"ch": q // plane[1], "sub": lax.rem(q, plane[1])}
+
+    barrier = pltpu.get_barrier_semaphore()
+    for i in range(1, peers):
+        pl.semaphore_signal(
+            barrier, inc=1, device_id=along(lax.rem(here + i, peers)), device_id_type=mesh_id
+        )
+    for i in range(1, fanout):
+        pl.semaphore_signal(
+            barrier, inc=1, device_id=beside(lax.rem(place + i, fanout)), device_id_type=mesh_id
+        )
+    pl.semaphore_wait(barrier, peers + fanout - 2)
+
+    def head_copy(kind, owner):
+        return pltpu.make_async_remote_copy(
+            src_ref=(power_head, rank_head)[kind].at[owner],
+            dst_ref=arrived.at[kind, owner],
+            send_sem=head_send.at[kind, owner],
+            recv_sem=head_recv.at[kind, owner],
+            device_id=along(lax.rem(here + peers - 1, peers)),
+            device_id_type=mesh_id,
+        )
+
+    def slot(kind, source):
+        return power_all.at[place, source] if kind == 0 else rank_owned.at[source]
+
+    def own_copy(kind, owner, source):
+        return pltpu.make_async_remote_copy(
+            src_ref=summed.at[kind, owner],
+            dst_ref=slot(kind, source),
+            send_sem=own_send.at[kind, owner],
+            recv_sem=own_recv.at[kind, source],
+            device_id=along(owner),
+            device_id_type=mesh_id,
+        )
+
+    def plane_copy(source, sender, target):
+        return pltpu.make_async_remote_copy(
+            src_ref=power_all.at[sender, source],
+            dst_ref=power_all.at[sender, source],
+            send_sem=plane_send.at[source, target],
+            recv_sem=plane_recv.at[source, sender],
+            device_id=beside(target),
+            device_id_type=mesh_id,
+        )
+
+    @pl.when(here > 0)
+    def _():
+        for kind in range(2):
+            for i in range(peers):
+                head_copy(kind, lax.rem(here + i, peers)).start()
+
+    transform(length, False, chunk, off_ref, grid_ref, back_ref, rank_ref, power_ref, acc, stage)
+
+    def total(kind, owner, out):
+        def own(l):
+            piece = stage[l + (0 if kind else per), pl.ds(owner * block * rows, block * rows), :]
+            return piece.reshape(block, rows, LANES)
+
+        @pl.when(here < peers - 1)
+        def _():
+            head_copy(kind, owner).wait_recv()
+            for l in range(per):
+                lanes = slice(l * LANES, (l + 1) * LANES)
+                late = arrived[kind, owner, :, :, lanes].astype(jnp.float32)
+                out[:, :, lanes] = (own(l) + late).astype(out.dtype)
+
+        @pl.when(here == peers - 1)
+        def _():
+            for l in range(per):
+                lanes = slice(l * LANES, (l + 1) * LANES)
+                out[:, :, lanes] = own(l).astype(out.dtype)
+
+    def forward(source):
+        for i in range(1, fanout):
+            plane_copy(source, place, lax.rem(place + i, fanout)).start()
+
+    for i in range(peers - 1):
+        owner = lax.rem(here + 1 + i, peers)
+        total(0, owner, summed.at[0, owner])
+        own_copy(0, owner, here).start()
+    total(0, here, slot(0, here))
+    forward(here)
+    for i in range(peers - 1):
+        owner = lax.rem(here + 1 + i, peers)
+        total(1, owner, summed.at[1, owner])
+        own_copy(1, owner, here).start()
+        source = lax.rem(here + peers - 1 - i, peers)
+        own_copy(0, owner, source).wait_recv()
+        forward(source)
+    total(1, here, slot(1, here))
+
+    for i in range(peers - 1):
+        owner = lax.rem(here + 1 + i, peers)
+        own_copy(1, owner, lax.rem(here + peers - 1 - i, peers)).wait_recv()
+        own_copy(0, owner, here).wait_send()
+        own_copy(1, owner, here).wait_send()
+    for z in range(peers):
+        for i in range(1, fanout):
+            other = lax.rem(place + i, fanout)
+            plane_copy(z, other, place).wait_recv()
+            plane_copy(z, place, other).wait_send()
+
+    @pl.when(here > 0)
+    def _():
+        for kind in range(2):
+            for i in range(peers):
+                head_copy(kind, lax.rem(here + i, peers)).wait_send()
+
+
+def transform_scratch(width, bins, segs):
+    return [
+        pltpu.VMEM((2 * width, 2 * bins), jnp.float32),
+        pltpu.VMEM((2 * width // LANES, bins * 2 * segs, LANES), jnp.float32),
+    ]
+
+
+def transform_cost(series, bins, segs, rows):
+    width, length = series.shape
+    return pl.CostEstimate(
+        flops=2 * segs * rows * 2 * bins * 2 * width,
+        bytes_accessed=2 * width * length * 2,
+        transcendentals=0,
+    )
+
+
+def head_spectra(offsets, grid, back, rank_series, power_series):
     width, length = rank_series.shape
     bins = grid.shape[-1]
     segs = offsets.shape[0]
-    back = waves_of(bin_index, -offsets, length)
-    dtype = jnp.bfloat16 if head else jnp.float32
-    out = jax.ShapeDtypeStruct((bins, 2 * segs, width), dtype)
-    rows = length if head else length // 2
+    peers = lax.axis_size("seg")
+    out = jax.ShapeDtypeStruct((peers, bins // peers, 2 * segs, width), jnp.bfloat16)
     vmem = pl.BlockSpec(memory_space=pltpu.VMEM)
     return pl.pallas_call(
-        functools.partial(spectra_kernel, length, head, 1024),
+        functools.partial(head_kernel, length, 1024),
         out_shape=(out, out),
-        in_specs=[pl.BlockSpec(memory_space=pltpu.SMEM), vmem, vmem, vmem, vmem],
+        in_specs=[pl.BlockSpec(memory_space=pltpu.SMEM)] + [vmem] * 4,
         out_specs=(vmem, vmem),
-        scratch_shapes=[
-            pltpu.VMEM((2 * width, 2 * bins), jnp.float32),
-            pltpu.VMEM((2 * width // LANES, bins * 2 * segs, LANES), jnp.float32),
+        scratch_shapes=transform_scratch(width, bins, segs),
+        compiler_params=pltpu.CompilerParams(vmem_limit_bytes=40 << 20),
+        cost_estimate=transform_cost(rank_series, bins, segs, length),
+        name="head_spectra",
+    )(offsets, grid, back, rank_series, power_series)
+
+
+def exchange(offsets, grid, back, rank_series, power_series, power_head, rank_head):
+    width, length = rank_series.shape
+    bins = grid.shape[-1]
+    segs = offsets.shape[0]
+    peers = lax.axis_size("seg")
+    plane = (lax.axis_size("ch"), lax.axis_size("sub"))
+    fanout = plane[0] * plane[1]
+    shape = (bins // peers, 2 * segs, width)
+    vmem = pl.BlockSpec(memory_space=pltpu.VMEM)
+    dma = pltpu.SemaphoreType.DMA
+    return pl.pallas_call(
+        functools.partial(exchange_kernel, length, 1024, peers, plane),
+        out_shape=(
+            jax.ShapeDtypeStruct((fanout, peers) + shape, jnp.bfloat16),
+            jax.ShapeDtypeStruct((peers,) + shape, jnp.bfloat16),
+        ),
+        in_specs=[pl.BlockSpec(memory_space=pltpu.SMEM)] + [vmem] * 6,
+        out_specs=(vmem, vmem),
+        scratch_shapes=transform_scratch(width, bins, segs)
+        + [
+            pltpu.VMEM((2, peers) + shape, jnp.bfloat16),
+            pltpu.VMEM((2, peers) + shape, jnp.bfloat16),
+            dma((2, peers)),
+            dma((2, peers)),
+            dma((2, peers)),
+            dma((2, peers)),
+            dma((peers, fanout)),
+            dma((peers, fanout)),
         ],
-        compiler_params=pltpu.CompilerParams(vmem_limit_bytes=40 << 20),
-        cost_estimate=pl.CostEstimate(
-            flops=2 * segs * rows * 2 * bins * 2 * width,
-            bytes_accessed=2 * width * length * 2,
-            transcendentals=0,
+        compiler_params=pltpu.CompilerParams(
+            vmem_limit_bytes=48 << 20, collective_id=0, has_side_effects=True
         ),
-        name="head_spectra" if head else "own_spectra",
-    )(offsets, grid, back, rank_series, power_series)
+        cost_estimate=transform_cost(rank_series, bins, segs, length // 2),
+        name="exchange_spectra",
+    )(offsets, grid, back, rank_series, power_series, power_head, rank_head)
 
 
 def cross_kernel(rank_ref, power_ref, out_ref):
@@ -153,26 +327,19 @@
     )(rank_owned, power_all)
 
 
-def to_owners(array):
-    peers = lax.axis_size("seg")
-    split = array.reshape((peers, array.shape[0] // peers) + array.shape[1:])
-    return lax.all_to_all(split, "seg", split_axis=0, concat_axis=0)
-
-
 def body(rank_series, power_series, seg_offsets, bin_index):
     length = rank_series.shape[1]
     coarse = jnp.arange(0, length, FINE, dtype=jnp.int32)
     samples = jnp.concatenate([coarse, jnp.arange(FINE, dtype=jnp.int32)])
     grid = waves_of(bin_index, samples, length)
     before = shifted(seg_offsets, "seg", 1)
-    rank_head, power_head = spectra(before, grid, bin_index, rank_series, power_series, True)
-    power_head = shifted(power_head, "seg", -1)
-    rank_head = shifted(rank_head, "seg", -1)
-    rank_own, power_own = spectra(seg_offsets, grid, bin_index, rank_series, power_series, False)
-    power_spectra = (power_own + power_head.astype(jnp.float32)).astype(jnp.bfloat16)
-    rank_spectra = (rank_own + rank_head.astype(jnp.float32)).astype(jnp.bfloat16)
-    power_all = lax.all_gather(to_owners(power_spectra), ("ch", "sub"), axis=0)
-    return cross(to_owners(rank_spectra), power_all)
+    back = waves_of(bin_index, -before, length)
+    power_head, rank_head = head_spectra(before, grid, back, rank_series, power_series)
+    back = waves_of(bin_index, -seg_offsets, length)
+    power_all, rank_owned = exchange(
+        seg_offsets, grid, back, rank_series, power_series, power_head, rank_head
+    )
+    return cross(rank_owned, power_all)
 
 
 def solution(mesh):

time: 116 us -> 92.3 us (0.80); the launches traced: 116 us -> 91.2 us
  Pallas kernels: 35.7 us -> 80.9 us
  blocking collectives: 32 us -> 0 us
  waiting for transfers between devices: 20.2 us -> 0.01 us
  between operations: 13.5 us -> 0.09 us
  starting transfers between devices: 7.5 us -> 4.92 us
  local copies, waits for them, and re-layouts: 5.43 us -> 3.85 us
    pallas_call x2, Pallas kernels: 18.5 us -> 63.6 us  [the longest x1 51.8 us: exchange(): pl.pallas_call(functools.partial(exchange_kernel, length, 1024, peers, pl...]
    all_to_all x2 -> x0, blocking collectives: 32 us -> none  [to_owners(): return lax.all_to_all(split, 'seg', split_axis=0, concat_axis=0)]
    ppermute x3 -> x1, waiting for transfers between devices: 20.2 us -> 0.01 us  [shifted(): return lax.ppermute(array, axis, pairs)]
    ppermute x3 -> x1, starting transfers between devices: 7.5 us -> 4.92 us  [shifted(): return lax.ppermute(array, axis, pairs)]
    unnamed x8, local copies, waits for them, and re-layouts: 4.77 us -> 3.18 us
  transfers between devices with their start and end apart: 4 -> 1, of which waited for: 2 -> 0; matrix products, arithmetic and copies ran while one was open for 2% -> 2% of each run, Pallas kernels for 6% -> 0%
where the time goes in v2:
time: 92.3 us; the launch traced here: 91.2 us
  Pallas kernels  80.9 us (88%)
  starting transfers between devices  4.92 us (5%)
  local copies, waits for them, and re-layouts  3.85 us (4%)
  other arithmetic  1.53 us (2%)
    pallas_call x1, Pallas kernels, exchange(): pl.pallas_call(functools.partial(exchange_kernel, length, 1024, peers, pl...  51.8 us
    pallas_call x1, Pallas kernels, cross(): pl.pallas_call(cross_kernel, out_shape=jax.ShapeDtypeStruct((2, bins, wid...  17.3 us
    pallas_call x1, Pallas kernels, head_spectra(): pl.pallas_call(functools.partial(head_kernel, length, 1024), out_shape=(o...  11.8 us
    ppermute x1, starting transfers between devices, shifted(): return lax.ppermute(array, axis, pairs)  4.92 us
    unnamed x8, local copies, waits for them, and re-layouts  3.18 us
  transfers between devices with their start and end apart: 1, of which 0 were waited for; matrix products, arithmetic and copies ran while one was open for 2% of the time, Pallas kernels for 0%

profile of v2, /device:TPU:0, one launch (start us, length us, event | category | flops | bytes accessed | tf_op | source)
XLA Modules:
  0.0 91.2 jit_solution(11541971889050837328)
XLA Ops:
  0.0 4.9 %collective-permute-start = (s32[4]{0:T(128)}, s32[4]{0:T(128)S(1)}, u32[]{:S(2)}, u32[]{:S(2)}) collective-permute-start(s32[4]{0:T(128)} %off_ref.1), channel_id=1, source_target_pairs={{0,4},{4,8},{8,12},{1,5},{5,9},{9,13},{2,6},{6,10},{10,14},{3,7},{... | collective-permute-start | bytes 56 | tf_op jit(solution)/shard_map/ppermute | solution.py:18
  4.9 0.7 neg.6
  5.6 0.1 pad_add_fusion
  5.7 0.7 stack.11
  6.3 0.6 fusion.4
  7.0 0.0 collective-permute-done.off_ref
  7.0 0.2 fusion.12
  7.2 0.0 copy-start
  7.2 1.6 %copy-done = bf16[256,4096]{1,0:T(8,128)(2,1)S(1)} copy-done((bf16[256,4096]{1,0:T(8,128)(2,1)S(1)}, bf16[256,4096]{1,0:T(8,128)(2,1)}, u32[]{:S(2)}) %copy-start) | copy-done | bytes 2097176
  8.8 0.0 copy-start.2
  8.8 1.6 %copy-done.2 = bf16[256,4096]{1,0:T(8,128)(2,1)S(1)} copy-done((bf16[256,4096]{1,0:T(8,128)(2,1)S(1)}, bf16[256,4096]{1,0:T(8,128)(2,1)}, u32[]{:S(2)}) %copy-start.2) | copy-done | bytes 2097176
  10.3 0.0 copy-start.1
  10.3 0.0 copy-start.3
  10.3 11.8 %head_spectra.1 = (bf16[4,32,8,256]{3,2,1,0:T(8,128)(2,1)S(1)}, bf16[4,32,8,256]{3,2,1,0:T(8,128)(2,1)S(1)}) custom-call(s32[4]{0:T(128)S(1)} %collective-permute-done.off_ref, f32[2,2,128,128]{3,2,1,0:T(8,128)S(1)} %pad_maximum_fusion.grid_ref, f32[2,2,4,128]{3,2,1,0:T(4,128)S(1)} %get-tuple-element.22.back_ref, bf16[256,4096]{1,0:T(8,128)(2,1)S(1)} %copy-done, ...), custom_call_target="tpu_custom_call" | custom-call | flops 4294967296 | bytes 4194304 | tf_op jit(solution)/shard_map/head_spectra/pallas_call | solution.py:241
  22.1 0.0 copy-done.1
  22.1 0.0 copy-done.3
  22.1 51.8 %exchange_spectra.1 = (bf16[4,4,32,8,256]{4,3,2,1,0:T(8,128)(2,1)S(1)}, bf16[4,32,8,256]{3,2,1,0:T(8,128)(2,1)S(1)}) custom-call(s32[4]{0:T(128)S(1)} %copy-done.3, f32[2,2,128,128]{3,2,1,0:T(8,128)S(1)} %pad_maximum_fusion.grid_ref, f32[2,2,4,128]{3,2,1,0:T(4,128)S(1)} %get-tuple-element.21.back_ref, bf16[256,4096]{1,0:T(8,128)(2,1)S(1)} %copy-done.1, ...), custom_call_target="tpu_custom_call" | custom-call | flops 2147483648 | bytes 4194304 | tf_op jit(solution)/shard_map/exchange_spectra/pallas_call | solution.py:263
  74.0 17.3 %cross_spectra.1 = bf16[2,32,256,1024]{3,2,1,0:T(8,128)(2,1)} custom-call(bf16[4,32,8,256]{3,2,1,0:T(8,128)(2,1)S(1)} %get-tuple-element.11.rank_ref, bf16[4,4,32,8,256]{4,3,2,1,0:T(8,128)(2,1)S(1)} %get-tuple-element.12.power_ref), custom_call_target="tpu_custom_call" | custom-call | tf_op jit(solution)/shard_map/cross_spectra/pallas_call | solution.py:316
  (5 shorter events, 0.0 us)
Async XLA Ops:
  0.0 7.0 %collective-permute-start = (s32[4]{0:T(128)}, s32[4]{0:T(128)S(1)}, u32[]{:S(2)}, u32[]{:S(2)}) collective-permute-start(s32[4]{0:T(128)} %off_ref.1), channel_id=1, source_target_pairs={{0,4},{4,8},{8,12},{1,5},{5,9},{9,13},{2,6},{6,10},{10,14},{3,7},{... | collective-permute-start | bytes 56 | tf_op jit(solution)/shard_map/ppermute | solution.py:18
  7.2 1.6 %copy-start = (bf16[256,4096]{1,0:T(8,128)(2,1)S(1)}, bf16[256,4096]{1,0:T(8,128)(2,1)}, u32[]{:S(2)}) copy-start(bf16[256,4096]{1,0:T(8,128)(2,1)} %rank_ref.3) | copy-start | bytes 6291460
  8.8 1.6 %copy-start.2 = (bf16[256,4096]{1,0:T(8,128)(2,1)S(1)}, bf16[256,4096]{1,0:T(8,128)(2,1)}, u32[]{:S(2)}) copy-start(bf16[256,4096]{1,0:T(8,128)(2,1)} %power_ref.3) | copy-start | bytes 6291460
  10.3 11.8 %copy-start.1 = (bf16[256,4096]{1,0:T(8,128)(2,1)S(1)}, bf16[256,4096]{1,0:T(8,128)(2,1)}, u32[]{:S(2)}) copy-start(bf16[256,4096]{1,0:T(8,128)(2,1)} %rank_ref.3) | copy-start | bytes 6291460
  10.3 11.8 %copy-start.3 = (s32[4]{0:T(128)S(1)}, s32[4]{0:T(128)}, u32[]{:S(2)}) copy-start(s32[4]{0:T(128)} %off_ref.1) | copy-start | bytes 52

commit v3 on v1

v3 whole, which is shorter than its diff:
```python
import functools
import math

import jax
import jax.numpy as jnp
from jax import lax
from jax.experimental import pallas as pl
from jax.experimental.pallas import tpu as pltpu
from jax.sharding import PartitionSpec as P

LANES = 128
FINE = 64


def waves_of(bin_index, samples, length):
    freqs = jnp.stack([bin_index, jnp.ones_like(bin_index)])
    phase = freqs[:, None, :] * samples[None, :, None] % length
    angle = 2.0 * math.pi / length * phase.astype(jnp.float32)
    return jnp.stack([jnp.cos(angle), jnp.sin(angle)])


def transform(length, head, chunk, grid_ref, back_ref, rank_ref, power_ref, acc, stage):
    bins = grid_ref.shape[-1]
    width = rank_ref.shape[0]
    segs = back_ref.shape[1]
    first = 0 if head else length // 2
    coarse = length // FINE
    factor = (3.0 * length / 8.0) ** (-0.5)

    for g in range(segs):
        acc[...] = jnp.zeros_like(acc)
        moved = []
        for kind in range(2):
            cb = grid_ref[0, kind, coarse : coarse + FINE, :]
            sb = grid_ref[1, kind, coarse : coarse + FINE, :]
            co = back_ref[kind, g : g + 1, :]
            so = back_ref[2 + kind, g : g + 1, :]
            moved.append((cb * co - sb * so, sb * co + cb * so))
        (cb, sb), (cv, sv) = moved
        cv, sv = cv * (0.5 * factor), sv * (0.5 * factor)
        nb, mb = -sb, -cb
        offset = back_ref[4, g : g + 1, :]
        within = lax.broadcasted_iota(jnp.int32, (FINE, bins), 0).astype(jnp.float32) - offset

        @pl.loop(0, (length - first) // chunk)
        def _(c):
            rows = []
            for piece in range(chunk // FINE):
                a = first // FINE + c * (chunk // FINE) + piece
                ca = grid_ref[0, 0, pl.ds(a, 1), :]
                sa = grid_ref[1, 0, pl.ds(a, 1), :]
                cw = grid_ref[0, 1, pl.ds(a, 1), :]
                sw = grid_ref[1, 1, pl.ds(a, 1), :]
                window = 0.5 * factor - (cw * cv - sw * sv)
                edge = -(a * FINE).astype(jnp.float32)
                inside = within < edge if head else within >= edge
                window = jnp.where(inside, window, 0.0)
                cosine = (ca * cb - sa * sb) * window
                sine = (sa * mb + ca * nb) * window
                rows.append(jnp.concatenate([cosine, sine], axis=1).astype(jnp.bfloat16))
            col = pl.multiple_of(first + c * chunk, chunk)
            series = jnp.concatenate(
                [rank_ref[:, pl.ds(col, chunk)], power_ref[:, pl.ds(col, chunk)]], axis=0
            )
            acc[...] += jnp.dot(
                series, jnp.concatenate(rows, axis=0), preferred_element_type=jnp.float32
            )

        for t in range(2):
            for l in range(2 * width // LANES):
                part = acc[l * LANES : (l + 1) * LANES, t * bins : (t + 1) * bins]
                stage[l, pl.ds(t * segs + g, bins, stride=2 * segs), :] = part.T


def exchange_kernel(
    length, chunk, peers, plane, grid_ref, back_ref, rank_hbm, power_hbm,
    power_all, rank_owned, acc, head_stage, own_stage, back_in, rank_ref, power_ref,
    near, from_above, from_below, summed,
    load_sem, back_sem, near_send, above_recv, below_recv, far_send, far_recv, plane_send, plane_recv,
):
    mesh_id = pl.DeviceIdType.MESH
    here = lax.axis_index("seg")
    above = lax.rem(here + 1, peers)
    below = lax.rem(here + peers - 1, peers)
    fanout = plane[0] * plane[1]
    place = lax.axis_index("ch") * plane[1] + lax.axis_index("sub")
    block, rows, width = summed.shape[2:]
    per = width // LANES
    inward = sorted(range(peers), key=lambda d: min(d, peers - 1 - d))

    loads = [
        pltpu.make_async_copy(rank_hbm, rank_ref, load_sem.at[0]),
        pltpu.make_async_copy(power_hbm, power_ref, load_sem.at[1]),
    ]
    for load in loads:
        load.start()

    def beside(q):
        return {"ch": q // plane[1], "sub": lax.rem(q, plane[1])}

    barrier = pltpu.get_barrier_semaphore()
    for i in range(1, peers):
        pl.semaphore_signal(
            barrier, inc=1, device_id={"seg": lax.rem(here + i, peers)}, device_id_type=mesh_id
        )
    for i in range(1, fanout):
        pl.semaphore_signal(
            barrier, inc=1, device_id=beside(lax.rem(place + i, fanout)), device_id_type=mesh_id
        )
    pl.semaphore_wait(barrier, peers + fanout - 2)

    back_copy = pltpu.make_async_remote_copy(
        src_ref=back_ref,
        dst_ref=back_in,
        send_sem=back_sem.at[0],
        recv_sem=back_sem.at[1],
        device_id={"seg": above},
        device_id_type=mesh_id,
    )

    def near_copy(kind, owner, up):
        return pltpu.make_async_remote_copy(
            src_ref=near.at[kind, owner],
            dst_ref=(from_below if up else from_above).at[kind, owner],
            send_sem=near_send.at[kind, owner],
            recv_sem=(below_recv if up else above_recv).at[kind, owner],
            device_id={"seg": above if up else below},
            device_id_type=mesh_id,
        )

    def slot(kind, group):
        return power_all.at[place, group] if kind == 0 else rank_owned.at[group]

    def far_copy(kind, owner, group):
        return pltpu.make_async_remote_copy(
            src_ref=summed.at[kind, owner],
            dst_ref=slot(kind, group),
            send_sem=far_send.at[kind, owner],
            recv_sem=far_recv.at[kind, group],
            device_id={"seg": owner},
            device_id_type=mesh_id,
        )

    def plane_copy(group, sender, target):
        return pltpu.make_async_remote_copy(
            src_ref=power_all.at[sender, group],
            dst_ref=power_all.at[sender, group],
            send_sem=plane_send.at[group, target],
            recv_sem=plane_recv.at[group, sender],
            device_id=beside(target),
            device_id_type=mesh_id,
        )

    def put(kind, owner, stage, late, out):
        for l in range(per):
            lanes = slice(l * LANES, (l + 1) * LANES)
            first = owner * block * rows
            piece = stage[l + (0 if kind else per), first : first + block * rows, :]
            piece = piece.reshape(block, rows, LANES)
            if late is not None:
                piece = piece + late[kind, owner, :, :, lanes].astype(jnp.float32)
            out[:, :, lanes] = piece.astype(out.dtype)

    def own_total(kind, owner, out):
        @pl.when(here < peers - 1)
        def _():
            near_copy(kind, owner, False).wait_recv()
            put(kind, owner, own_stage, from_above, out)

        @pl.when(here == peers - 1)
        def _():
            put(kind, owner, own_stage, None, out)

    def head_total(kind, owner, out):
        near_copy(kind, owner, True).wait_recv()
        put(kind, owner, head_stage, from_below, out)

    def forward(group):
        for i in range(1, fanout):
            plane_copy(group, place, lax.rem(place + i, fanout)).start()

    @pl.when(here < peers - 1)
    def _():
        back_copy.start()

    for load in loads:
        load.wait()

    @pl.when(here > 0)
    def _():
        back_copy.wait_recv()
        transform(length, True, chunk, grid_ref, back_in, rank_ref, power_ref, acc, head_stage)
        for kind in range(2):
            for d in range(peers - 1):
                @pl.when(d < here)
                def _():
                    put(kind, d, head_stage, None, near.at[kind, d])
                    near_copy(kind, d, False).start()

    transform(length, False, chunk, grid_ref, back_ref, rank_ref, power_ref, acc, own_stage)
    for kind in range(2):
        for d in reversed(range(1, peers)):
            @pl.when(d > here)
            def _():
                put(kind, d, own_stage, None, near.at[kind, d])
                near_copy(kind, d, True).start()

    for kind in range(2):
        for d in inward:
            @pl.when(d < here)
            def _():
                own_total(kind, d, summed.at[kind, d])
                far_copy(kind, d, here).start()

            @pl.when((d > here) & (here > 0))
            def _():
                head_total(kind, d, summed.at[kind, d])
                far_copy(kind, d, below).start()

        for d in range(peers):
            @pl.when(d == here)
            def _():
                own_total(kind, d, slot(kind, d))
                if kind == 0:
                    forward(d)
                if d > 0:
                    head_total(kind, d, slot(kind, d - 1))
                    if kind == 0:
                        forward(d - 1)

    def apart(group):
        return (group != here) & (group != here - 1)

    for group in reversed(inward):
        @pl.when(apart(group))
        def _():
            far_copy(0, here, group).wait_recv()
            forward(group)

    for group in range(peers):
        @pl.when(apart(group))
        def _():
            far_copy(1, here, group).wait_recv()

        for i in range(1, fanout):
            other = lax.rem(place + i, fanout)
            plane_copy(group, other, place).wait_recv()
            plane_copy(group, place, other).wait_send()

    for kind in range(2):
        for d in range(peers):
            @pl.when(d != here)
            def _():
                near_copy(kind, d, True).wait_send()

            @pl.when((d < here) | ((d > here) & (here > 0)))
            def _():
                far_copy(kind, d, 0).wait_send()

    @pl.when(here < peers - 1)
    def _():
        back_copy.wait_send()


def exchange(grid, back, rank_series, power_series):
    width, length = rank_series.shape
    bins = grid.shape[-1]
    segs = back.shape[1]
    peers = lax.axis_size("seg")
    plane = (lax.axis_size("ch"), lax.axis_size("sub"))
    fanout = plane[0] * plane[1]
    shape = (bins // peers, 2 * segs, width)
    vmem = pl.BlockSpec(memory_space=pltpu.VMEM)
    hbm = pl.BlockSpec(memory_space=pl.ANY)
    dma = pltpu.SemaphoreType.DMA
    stage = pltpu.VMEM((2 * width // LANES, bins * 2 * segs, LANES), jnp.float32)
    return pl.pallas_call(
        functools.partial(exchange_kernel, length, 1024, peers, plane),
        out_shape=(
            jax.ShapeDtypeStruct((fanout, peers) + shape, jnp.bfloat16),
            jax.ShapeDtypeStruct((peers,) + shape, jnp.bfloat16),
        ),
        in_specs=[vmem, vmem, hbm, hbm],
        out_specs=(vmem, vmem),
        scratch_shapes=[
            pltpu.VMEM((2 * width, 2 * bins), jnp.float32),
            stage,
            stage,
            pltpu.VMEM(back.shape, jnp.float32),
            pltpu.VMEM(rank_series.shape, jnp.bfloat16),
            pltpu.VMEM(power_series.shape, jnp.bfloat16),
        ]
        + [pltpu.VMEM((2, peers) + shape, jnp.bfloat16)] * 4
        + [dma((2,)), dma((2,))]
        + [dma((2, peers))] * 5
        + [dma((peers, fanout))] * 2,
        compiler_params=pltpu.CompilerParams(
            vmem_limit_bytes=56 << 20, collective_id=0, has_side_effects=True
        ),
        name="exchange_spectra",
    )(grid, back, rank_series, power_series)


def cross_kernel(rank_ref, power_ref, out_ref):
    peers, block, rows, width = rank_ref.shape
    gathered = power_ref.shape[0]
    half = rows // 2
    depth = peers * rows
    for i in range(block):
        rank = rank_ref[:, i].astype(jnp.float32)
        turned = jnp.concatenate([-rank[:, half:], rank[:, :half]], axis=1)
        both = jnp.concatenate([rank.reshape(depth, width), turned.reshape(depth, width)], axis=1)
        both = both.astype(jnp.bfloat16)
        for d in range(gathered):
            power = power_ref[d, :, i].astype(jnp.float32).reshape(depth, width)
            sums = lax.dot_general(
                both,
                power.astype(jnp.bfloat16),
                (((0,), (0,)), ((), ())),
                preferred_element_type=jnp.float32,
            ).astype(out_ref.dtype)
            out_ref[0, i, :, d * width : (d + 1) * width] = sums[:width]
            out_ref[1, i, :, d * width : (d + 1) * width] = sums[width:]


def cross(rank_owned, power_all):
    peers, bins, rows, width = rank_owned.shape
    gathered = power_all.shape[0]
    block = 2
    return pl.pallas_call(
        cross_kernel,
        out_shape=jax.ShapeDtypeStruct((2, bins, width, gathered * width), jnp.bfloat16),
        grid=(bins // block,),
        in_specs=[
            pl.BlockSpec((peers, block, rows, width), lambda k: (0, k, 0, 0)),
            pl.BlockSpec((gathered, peers, block, rows, width), lambda k: (0, 0, k, 0, 0)),
        ],
        out_specs=pl.BlockSpec((2, block, width, gathered * width), lambda k: (0, k, 0, 0)),
        compiler_params=pltpu.CompilerParams(vmem_limit_bytes=48 << 20),
        name="cross_spectra",
    )(rank_owned, power_all)


def body(rank_series, power_series, seg_offsets, bin_index):
    length = rank_series.shape[1]
    coarse = jnp.arange(0, length, FINE, dtype=jnp.int32)
    samples = jnp.concatenate([coarse, jnp.arange(FINE, dtype=jnp.int32)])
    grid = waves_of(bin_index, samples, length)
    back = waves_of(bin_index, -seg_offsets, length).reshape(4, -1, bin_index.shape[0])
    offset_rows = jnp.broadcast_to(seg_offsets.astype(jnp.float32)[None, :, None], (1,) + back.shape[1:])
    back = jnp.concatenate([back, offset_rows])
    power_all, rank_owned = exchange(grid, back, rank_series, power_series)
    return cross(rank_owned, power_all)


def solution(mesh):
    return jax.shard_map(
        body,
        mesh=mesh,
        in_specs=(
            P(("groups", "ch", "sub"), "seg"),
            P(("groups", "ch", "sub"), "seg"),
            P(("groups", "seg")),
            P(),
        ),
        out_specs=P(None, ("groups", "seg"), ("ch", "sub"), None),
        check_vma=False,
    )
```

time: 116 us -> 78.9 us (0.68)
  the two profiles are of different devices: /device:TPU:0 before, /device:TPU:23 now
where the time goes in v3:
time: 78.9 us; the launch traced here: 78.7 us
  Pallas kernels  72.4 us (92%)
  local copies, waits for them, and re-layouts  3.36 us (4%)
  other arithmetic  2.86 us (4%)
    pallas_call x1, Pallas kernels, exchange(): pl.pallas_call(functools.partial(exchange_kernel, length, 1024, peers, pl...  55.2 us
    pallas_call x1, Pallas kernels, cross(): pl.pallas_call(cross_kernel, out_shape=jax.ShapeDtypeStruct((2, bins, wid...  17.3 us
    unnamed x4, local copies, waits for them, and re-layouts  2.63 us

profile of v3, /device:TPU:23, one launch (start us, length us, event | category | flops | bytes accessed | tf_op | source)
XLA Modules:
  0.0 78.7 jit_solution(14875012182207601058)
XLA Ops:
  0.0 0.1 pad_add_fusion
  0.1 0.7 stack.9
  0.7 0.7 fusion.10
  1.5 0.1 broadcast_in_dim.2
  1.5 0.1 fusion.9
  1.7 0.6 pad_maximum_fusion.1.back_ref
  2.3 0.6 fusion.4
  2.9 0.7 pad_maximum_fusion.grid_ref
  3.6 55.2 %exchange_spectra.1 = (bf16[4,4,32,8,256]{4,3,2,1,0:T(8,128)(2,1)}, bf16[4,32,8,256]{3,2,1,0:T(8,128)(2,1)}) custom-call(f32[2,2,128,128]{3,2,1,0:T(8,128)} %pad_maximum_fusion.grid_ref, f32[5,4,128]{2,1,0:T(4,128)} %pad_maximum_fusion.1.back_ref, bf16[256,4096]{1,0:T(8,128)(2,1)} %rank_hbm.1, bf16[256,4096]{1,0:T(8,128)(2,1)} %power_hbm.1), custom_call_target="tpu_custom_call" | custom-call | tf_op jit(solution)/shard_map/exchange_spectra/pallas_call | solution.py:277
  58.8 0.0 copy-start
  58.8 1.6 %copy-done = bf16[4,4,32,8,256]{4,3,2,1,0:T(8,128)(2,1)S(1)} copy-done((bf16[4,4,32,8,256]{4,3,2,1,0:T(8,128)(2,1)S(1)}, bf16[4,4,32,8,256]{4,3,2,1,0:T(8,128)(2,1)}, u32[]{:S(2)}) %copy-start) | copy-done | bytes 2097176
  60.4 0.0 copy-start.1
  60.4 1.0 %copy-done.1 = bf16[4,32,8,256]{3,2,1,0:T(8,128)(2,1)S(1)} copy-done((bf16[4,32,8,256]{3,2,1,0:T(8,128)(2,1)S(1)}, bf16[4,32,8,256]{3,2,1,0:T(8,128)(2,1)}, u32[]{:S(2)}) %copy-start.1) | copy-done | bytes 524312
  61.4 17.3 %cross_spectra.1 = bf16[2,32,256,1024]{3,2,1,0:T(8,128)(2,1)} custom-call(bf16[4,32,8,256]{3,2,1,0:T(8,128)(2,1)S(1)} %copy-done.1, bf16[4,4,32,8,256]{4,3,2,1,0:T(8,128)(2,1)S(1)} %copy-done), custom_call_target="tpu_custom_call" | custom-call | tf_op jit(solution)/shard_map/cross_spectra/pallas_call | solution.py:330
  (3 shorter events, 0.0 us)
Async XLA Ops:
  58.8 1.6 %copy-start = (bf16[4,4,32,8,256]{4,3,2,1,0:T(8,128)(2,1)S(1)}, bf16[4,4,32,8,256]{4,3,2,1,0:T(8,128)(2,1)}, u32[]{:S(2)}) copy-start(bf16[4,4,32,8,256]{4,3,2,1,0:T(8,128)(2,1)} %get-tuple-element.8.power_ref) | copy-start | bytes 6291460
  60.4 1.0 %copy-start.1 = (bf16[4,32,8,256]{3,2,1,0:T(8,128)(2,1)S(1)}, bf16[4,32,8,256]{3,2,1,0:T(8,128)(2,1)}, u32[]{:S(2)}) copy-start(bf16[4,32,8,256]{3,2,1,0:T(8,128)(2,1)} %get-tuple-element.7.rank_ref) | copy-start | bytes 1572868
